TPU v7x, 32 devices: a whole 2x2x4 slice. The times are simulated.
32 devices in a mesh: ax: 8 (over z, x), sec: 4 (over y, core).
Axes of the slice: x: 2, y: 2, z: 4, core: 2. Of those that a mesh axis runs over, the one named last changes fastest.
Arguments:
- density: float32 [16, 256, 512], P('ax', None, 'sec'), may hold values from 0.7 to 1.4
- velocity: float32 [3, 16, 256, 512], P(None, 'ax', None, 'sec'), may hold values from -2.5 to 2.5
- pressure: float32 [16, 256, 512], P('ax', None, 'sec'), may hold values from 0.6 to 1.6
- cutoff: int32 [64], replicated, may hold values from 2 to 129, as said below
Outputs:
- density_new: float32 [16, 256, 512], P('ax', None, 'sec')
- velocity_new: float32 [3, 16, 256, 512], P(None, 'ax', None, 'sec')
- pressure_new: float32 [16, 256, 512], P('ax', None, 'sec')
Inputs may be any that keep to these rules, and one draw needn't show every extreme that they name: cutoff[j] is the number of azimuthal modes kept in cycle j.
All inputs are finite; a program needn't handle non-finite values.
Results may differ from a plain program's by a relative error of at most 0.00005.
Values sent between devices are 32-bit elements; how exact they have to be, the bound alone decides.
A program may use at most 64 MiB of HBM per device.

v0:
```python
import functools
import math

import jax
import jax.numpy as jnp
import numpy as np
from jax import lax
from jax.experimental import pallas as pl
from jax.experimental.pallas import tpu as pltpu
from jax.sharding import PartitionSpec as P

MESH = pl.DeviceIdType.MESH
PAD = 8
SUB = 32


def tables(points, local, modes):
    width = -(-(2 * modes - 1) // 128) * 128
    mode = np.zeros(width, np.int64)
    mode[:modes] = np.arange(modes)
    mode[modes : 2 * modes - 1] = np.arange(1, modes)

    def rows(index):
        angle = 2.0 * np.pi / points * ((index[:, None] * mode[None, :]) % points)
        out = np.where(np.arange(width) < modes, np.cos(angle), np.sin(angle))
        out[:, 2 * modes - 1 :] = 0.0
        return out

    sectors = points // local
    forward = rows(np.arange(points)).reshape(sectors, local, width)
    inverse = np.zeros((sectors, width, 2 * local))
    for s in range(sectors):
        inverse[s, :, :local] = forward[s].T
        edges = rows(np.array([s * local - 1, (s + 1) * local]) % points)
        inverse[s, :, local] = edges[0]
        inverse[s, :, 2 * local - 1] = edges[1]
    scale = np.where(mode == 0, 1.0, 2.0) / points
    scale[2 * modes - 1 :] = 0.0
    return (
        forward.astype(np.float32),
        inverse.astype(np.float32),
        mode.astype(np.int32),
        scale.astype(np.float32),
    )


def kernel(
    spacing, angle_step, inner,
    dens, velo, pres, weight, forward, inverse,
    dens_out, velo_out, pres_out,
    start, section, edge, x_low, x_high, gathered, pack, from_left, from_right, inv_r,
    gather_send, gather_recv, x_send, x_recv, t_send, t_recv,
):
    rows, local = dens.shape[1], dens.shape[2]
    chunks = rows // inner
    tau = 0.05 * spacing
    ax, n_ax = lax.axis_index("ax"), lax.axis_size("ax")
    me = lax.axis_index("sec")
    before, after = lax.rem(ax + n_ax - 1, n_ax), lax.rem(ax + 1, n_ax)
    left, right = lax.rem(me + 3, 4), lax.rem(me + 1, 4)
    mate = me + 1 - 2 * lax.rem(me, 2)
    opposite = lax.rem(me + 2, 4)
    far = lax.rem(mate + 2, 4)

    barrier = pltpu.get_barrier_semaphore()
    for target in ({"ax": before}, {"ax": after}, {"sec": mate}, {"sec": opposite}, {"sec": far}):
        pl.semaphore_signal(barrier, inc=1, device_id=target, device_id_type=MESH)
    pl.semaphore_wait(barrier, 5)

    def remote(src, dst, send, recv, target):
        return pltpu.make_async_remote_copy(
            src_ref=src, dst_ref=dst, send_sem=send, recv_sem=recv,
            device_id=target, device_id_type=MESH,
        )

    def x_copies(state, stage, c):
        here, there = pl.ds(PAD + c * inner, inner), pl.ds(c * inner, inner)
        return (
            remote(state.at[:, 0, here], x_high.at[stage, :, there],
                   x_send.at[stage, c, 0], x_recv.at[stage, c, 0], {"ax": before}),
            remote(state.at[:, 1, here], x_low.at[stage, :, there],
                   x_send.at[stage, c, 1], x_recv.at[stage, c, 1], {"ax": after}),
        )

    def t_copies(stage, c):
        return (
            remote(pack.at[stage, c - 1], from_right.at[stage, c - 1],
                   t_send.at[stage, c, 0], t_recv.at[stage, c, 0], {"sec": left}),
            remote(pack.at[stage, c - 1], from_left.at[stage, c - 1],
                   t_send.at[stage, c, 1], t_recv.at[stage, c, 1], {"sec": right}),
        )

    def gather_copies(stage, p):
        own = gathered.at[stage, 0, p]
        arrived = gathered.at[stage, 2, p]
        return (
            remote(own, arrived, gather_send.at[stage, p, 0], gather_recv.at[stage, p, 0],
                   {"sec": opposite}),
            remote(own, gathered.at[stage, 1, p], gather_send.at[stage, p, 1],
                   gather_recv.at[stage, p, 1], {"sec": mate}),
            remote(arrived, gathered.at[stage, 3, p], gather_send.at[stage, p, 2],
                   gather_recv.at[stage, p, 2], {"sec": mate}),
        )

    lane = lax.broadcasted_iota(jnp.int32, (inner, local), 1)

    def send_chunk(state, stage, c):
        for copy in x_copies(state, stage, c):
            copy.start()
        packed = jnp.zeros((inner, local), jnp.float32)
        for f in range(5):
            for p in range(2):
                k = 2 * f + p
                value = state[f, p, PAD + c * inner : PAD + (c + 1) * inner]
                packed = jnp.where(lane == k, pltpu.roll(value, (k + 1) % local, 1), packed)
                packed = jnp.where(lane == 10 + k, pltpu.roll(value, 10 + k, 1), packed)
        pack[stage, c - 1] = packed
        for copy in t_copies(stage, c):
            copy.start()

    def receive_edges(stage, c):
        for copy in t_copies(stage, c):
            copy.wait_recv()
        low, high = from_left[stage, c - 1], from_right[stage, c - 1]
        for f in range(5):
            for p in range(2):
                k = 2 * f + p
                a = pltpu.roll(low, (local - k) % local, 1)
                b = pltpu.roll(high, local - 1 - (10 + k), 1)
                edge[f, p, c * inner : (c + 1) * inner] = jnp.where(lane == 0, a, b)

    def send_inner(stage, p):
        first, second, _ = gather_copies(stage, p)
        first.start()
        second.start()

    def filter_inner(state, stage):
        for p in range(2):
            first, _, third = gather_copies(stage, p)
            first.wait_recv()
            third.start()
        for p in range(2):
            gather_copies(stage, p)[1].wait_recv()
            gather_copies(stage, p)[2].wait_recv()
            coeffs = None
            for slots, owners in (((0, 1), (me, mate)), ((2, 3), (opposite, far))):
                values = jnp.concatenate([gathered[stage, slots[0], p], gathered[stage, slots[1], p]], axis=1)
                basis = jnp.concatenate([forward[owners[0]], forward[owners[1]]], axis=0)
                part = jnp.dot(values, basis, precision=lax.Precision.HIGHEST, preferred_element_type=jnp.float32)
                coeffs = part if coeffs is None else coeffs + part
            coeffs = coeffs.reshape(5, inner, -1) * weight[...][None]
            flat = coeffs.reshape(5 * inner, -1)
            both = jnp.dot(flat, inverse[me], precision=lax.Precision.HIGHEST, preferred_element_type=jnp.float32)
            across = jnp.dot(coeffs[:, :8].reshape(40, -1), inverse[opposite, :, :local],
                             precision=lax.Precision.HIGHEST, preferred_element_type=jnp.float32)
            for f in range(5):
                state[f, p, PAD : PAD + inner] = both[f * inner : (f + 1) * inner, :local]
                edge[f, p, 0:inner] = both[f * inner : (f + 1) * inner, local:]
                row = across[8 * f : 8 * f + 1]
                state[f, p, PAD - 1 : PAD] = -row if f in (2, 3) else row
        for copy in x_copies(state, stage, 0):
            copy.start()

    def wall(state):
        for f in range(5):
            for p in range(2):
                row = state[f, p, PAD + rows - 1 : PAD + rows]
                state[f, p, PAD + rows : PAD + rows + 1] = -row if f == 2 else row

    sub_lane = lax.broadcasted_iota(jnp.int32, (SUB, local), 1)

    def advance(state, stage, p, r0):
        here = slice(PAD + r0, PAD + r0 + SUB)
        plain = slice(r0, r0 + SUB)
        s = [state[f, p, here] for f in range(5)]
        over_r = inv_r[plain]
        over_rho = 1.0 / s[0]
        u, v, w = s[1], s[2], s[3]

        def grads(f):
            if p == 0:
                gx = state[f, 1, here] - x_low[stage, f, plain]
            else:
                gx = x_high[stage, f, plain] - state[f, 0, here]
            gr = state[f, p, PAD + r0 + 1 : PAD + r0 + 1 + SUB] - state[f, p, PAD + r0 - 1 : PAD + r0 - 1 + SUB]
            border = edge[f, p, plain]
            ahead = jnp.where(sub_lane == local - 1, border, pltpu.roll(s[f], local - 1, 1))
            behind = jnp.where(sub_lane == 0, border, pltpu.roll(s[f], 1, 1))
            gt = (ahead - behind) * ((0.5 / angle_step) * over_r)
            return gx * (0.5 / spacing), gr * (0.5 / spacing), gt

        g = [grads(f) for f in range(5)]
        advect = [u * gx + v * gr + w * gt for gx, gr, gt in g]
        diverg = g[1][0] + g[2][1] + v * over_r + g[3][2]
        rates = (
            -advect[0] - s[0] * diverg,
            -advect[1] - g[4][0] * over_rho,
            -advect[2] + w * w * over_r - g[4][1] * over_rho,
            -advect[3] - v * w * over_r - g[4][2] * over_rho,
            -advect[4] - 1.4 * s[4] * diverg,
        )
        return s, [tau * rate for rate in rates]

    for p in range(2):
        for f in range(5):
            source = dens if f == 0 else pres if f == 4 else velo.at[f - 1]
            gathered[0, 0, p, f * inner : (f + 1) * inner] = source[p, 0:inner]
        send_inner(0, p)
    for c in range(1, chunks):
        span = slice(c * inner, (c + 1) * inner)
        for f in range(5):
            source = dens if f == 0 else pres if f == 4 else velo.at[f - 1]
            start[f, :, PAD + c * inner : PAD + (c + 1) * inner] = source[:, span]
        send_chunk(start, 0, c)
    wall(start)
    radius = (lax.broadcasted_iota(jnp.int32, (rows, local), 0).astype(jnp.float32) + 0.5) * spacing
    inv_r[...] = 1.0 / radius
    filter_inner(start, 0)

    order = list(range(1, chunks)) + [0]
    for c in order:
        for copy in x_copies(start, 0, c):
            copy.wait_recv()
        if c > 0:
            receive_edges(0, c)
        for p in range(2):
            for r0 in range(c * inner, (c + 1) * inner, SUB):
                s, step = advance(start, 0, p, r0)
                for f in range(5):
                    if c > 0:
                        section[f, p, PAD + r0 : PAD + r0 + SUB] = s[f] + step[f]
                    else:
                        gathered[1, 0, p, f * inner + r0 : f * inner + r0 + SUB] = s[f] + step[f]
            if c == 0:
                send_inner(1, p)
        if c > 0:
            send_chunk(section, 1, c)
    wall(section)
    filter_inner(section, 1)

    for c in order:
        for copy in x_copies(section, 1, c):
            copy.wait_recv()
        if c > 0:
            receive_edges(1, c)
        for p in range(2):
            for r0 in range(c * inner, (c + 1) * inner, SUB):
                s, step = advance(section, 1, p, r0)
                for f in range(5):
                    value = 0.5 * start[f, p, PAD + r0 : PAD + r0 + SUB] + 0.5 * (s[f] + step[f])
                    target = dens_out if f == 0 else pres_out if f == 4 else velo_out.at[f - 1]
                    target[p, r0 : r0 + SUB] = value

    for stage, state in ((0, start), (1, section)):
        for c in range(chunks):
            for copy in x_copies(state, stage, c):
                copy.wait_send()
            if c > 0:
                for copy in t_copies(stage, c):
                    copy.wait_send()
        for p in range(2):
            for copy in gather_copies(stage, p):
                copy.wait_send()


def body(density, velocity, pressure, cutoff):
    planes, rows, local = density.shape
    points = local * lax.axis_size("sec")
    inner = rows // 4
    forward, inverse, mode, scale = tables(points, local, 2 * inner + 1)
    weight = jnp.where(mode[None, :] < cutoff[:, None], scale[None, :], 0.0).astype(jnp.float32)
    f32 = jnp.float32
    outer_chunks = rows // inner - 1
    vmem = pl.BlockSpec(memory_space=pltpu.VMEM)
    run = pl.pallas_call(
        functools.partial(kernel, 1.0 / rows, 2.0 * math.pi / points, inner),
        out_shape=(
            jax.ShapeDtypeStruct(density.shape, f32),
            jax.ShapeDtypeStruct(velocity.shape, f32),
            jax.ShapeDtypeStruct(pressure.shape, f32),
        ),
        in_specs=[vmem] * 6,
        out_specs=(vmem,) * 3,
        scratch_shapes=[
            pltpu.VMEM((5, planes, rows + 2 * PAD, local), f32),
            pltpu.VMEM((5, planes, rows + 2 * PAD, local), f32),
            pltpu.VMEM((5, planes, rows, local), f32),
            pltpu.VMEM((2, 5, rows, local), f32),
            pltpu.VMEM((2, 5, rows, local), f32),
            pltpu.VMEM((2, 4, planes, 5 * inner, local), f32),
            pltpu.VMEM((2, outer_chunks, inner, local), f32),
            pltpu.VMEM((2, outer_chunks, inner, local), f32),
            pltpu.VMEM((2, outer_chunks, inner, local), f32),
            pltpu.VMEM((rows, local), f32),
            pltpu.SemaphoreType.DMA((2, planes, 3)),
            pltpu.SemaphoreType.DMA((2, planes, 3)),
            pltpu.SemaphoreType.DMA((2, outer_chunks + 1, 2)),
            pltpu.SemaphoreType.DMA((2, outer_chunks + 1, 2)),
            pltpu.SemaphoreType.DMA((2, outer_chunks + 1, 2)),
            pltpu.SemaphoreType.DMA((2, outer_chunks + 1, 2)),
        ],
        compiler_params=pltpu.CompilerParams(
            collective_id=0, has_side_effects=True, vmem_limit_bytes=48 * 1024 * 1024
        ),
    )
    return run(density, velocity, pressure, weight, jnp.asarray(forward), jnp.asarray(inverse))


def solution(mesh):
    return jax.shard_map(
        body,
        mesh=mesh,
        in_specs=(P("ax", None, "sec"), P(None, "ax", None, "sec"), P("ax", None, "sec"), P()),
        out_specs=(P("ax", None, "sec"), P(None, "ax", None, "sec"), P("ax", None, "sec")),
        check_vma=False,
    )
```

profile of v0, /device:TPU:0, one launch (start us, length us, event | category | flops | bytes accessed | tf_op | source)
XLA Modules:
  0.0 77.6 jit_solution(6225495191917410756)
XLA Ops:
  0.6 0.8 %compare_select_fusion.weight = f32[64,384]{1,0:T(8,128)S(1)} fusion(f32[384]{0:T(512)} %constant.18, s32[384]{0:T(512)} %constant.17, s32[64]{0:T(128)} %param.11), kind=kLoop, calls=%fused_computation | loop fusion | flops 49152 | bytes 101632 | tf_op jit(solution)/shard_map/jit(_where)/select_n | solution.py:271
  1.4 0.0 copy-start
  1.4 1.4 %copy-done = f32[4,384,256]{2,1,0:T(8,128)S(1)} copy-done((f32[4,384,256]{2,1,0:T(8,128)S(1)}, f32[4,384,256]{2,1,0:T(8,128)}, u32[]{:S(2)}) %copy-start) | copy-done | bytes 1572888
  2.8 0.0 copy-start.1
  2.8 1.1 %copy-done.1 = f32[3,2,256,128]{3,2,1,0:T(8,128)S(1)} copy-done((f32[3,2,256,128]{3,2,1,0:T(8,128)S(1)}, f32[3,2,256,128]{3,2,1,0:T(8,128)}, u32[]{:S(2)}) %copy-start.1) | copy-done | bytes 786456
  4.0 0.0 copy-start.2
  4.0 1.1 %copy-done.2 = f32[4,128,384]{2,1,0:T(8,128)S(1)} copy-done((f32[4,128,384]{2,1,0:T(8,128)S(1)}, f32[4,128,384]{2,1,0:T(8,128)}, u32[]{:S(2)}) %copy-start.2) | copy-done | bytes 786456
  5.1 0.0 copy-start.3
  5.1 0.9 %copy-done.3 = f32[2,256,128]{2,1,0:T(8,128)S(1)} copy-done((f32[2,256,128]{2,1,0:T(8,128)S(1)}, f32[2,256,128]{2,1,0:T(8,128)}, u32[]{:S(2)}) %copy-start.3) | copy-done | bytes 262168
  6.0 0.0 copy-start.4
  6.0 0.9 %copy-done.4 = f32[2,256,128]{2,1,0:T(8,128)S(1)} copy-done((f32[2,256,128]{2,1,0:T(8,128)S(1)}, f32[2,256,128]{2,1,0:T(8,128)}, u32[]{:S(2)}) %copy-start.4) | copy-done | bytes 262168
  7.0 68.3 %shard_map.103 = (f32[2,256,128]{2,1,0:T(8,128)S(1)}, f32[3,2,256,128]{3,2,1,0:T(8,128)S(1)}, f32[2,256,128]{2,1,0:T(8,128)S(1)}) custom-call(f32[2,256,128]{2,1,0:T(8,128)S(1)} %copy-done.3, f32[3,2,256,128]{3,2,1,0:T(8,128)S(1)} %copy-done.1, f32[2,256,128]{2,1,0:T(8,128)S(1)} %copy-done.4, f32[64,384]{1,0:T(8,128)S(1)} %compare_select_fusion.weight, ...), custom_call_target="tpu_custom_call" | custom-call | tf_op jit(solution)/shard_map/pallas_call | solution.py:306
  75.3 0.7 copy.14
  76.0 0.9 %copy.15 = f32[3,2,256,128]{3,2,1,0:T(8,128)} copy(f32[3,2,256,128]{3,2,1,0:T(8,128)S(1)} %get-tuple-element.7) | data formatting | bytes 1572864
  76.9 0.7 copy.16
Async XLA Ops:
  1.4 1.4 %copy-start = (f32[4,384,256]{2,1,0:T(8,128)S(1)}, f32[4,384,256]{2,1,0:T(8,128)}, u32[]{:S(2)}) copy-start(f32[4,384,256]{2,1,0:T(8,128)} %constant.13.clone.inverse) | copy-start | bytes 4718596
  2.8 1.1 %copy-start.1 = (f32[3,2,256,128]{3,2,1,0:T(8,128)S(1)}, f32[3,2,256,128]{3,2,1,0:T(8,128)}, u32[]{:S(2)}) copy-start(f32[3,2,256,128]{3,2,1,0:T(8,128)} %velo.1) | copy-start | bytes 2359300
  4.0 1.1 %copy-start.2 = (f32[4,128,384]{2,1,0:T(8,128)S(1)}, f32[4,128,384]{2,1,0:T(8,128)}, u32[]{:S(2)}) copy-start(f32[4,128,384]{2,1,0:T(8,128)} %constant.12.clone.forward) | copy-start | bytes 2359300
  5.1 0.9 %copy-start.3 = (f32[2,256,128]{2,1,0:T(8,128)S(1)}, f32[2,256,128]{2,1,0:T(8,128)}, u32[]{:S(2)}) copy-start(f32[2,256,128]{2,1,0:T(8,128)} %dens.1) | copy-start | bytes 786436
  6.0 0.9 %copy-start.4 = (f32[2,256,128]{2,1,0:T(8,128)S(1)}, f32[2,256,128]{2,1,0:T(8,128)}, u32[]{:S(2)}) copy-start(f32[2,256,128]{2,1,0:T(8,128)} %pres.1) | copy-start | bytes 786436
where the time goes:
time: 77.9 us; the launch traced here: 77.6 us
  Pallas kernels  68.3 us (88%)
  local copies, waits for them, and re-layouts  7.85 us (10%)
  other arithmetic  0.78 us (1%)
    pallas_call x1, Pallas kernels, body(): run(density, velocity, pressure, weight, jnp.asarray(forward), jnp.asarra...  68.3 us
    unnamed x13, local copies, waits for them, and re-layouts  7.85 us

commit v1 on v0

v1 whole, which is shorter than its diff:
```python
import functools
import math

import jax
import jax.numpy as jnp
import numpy as np
from jax import lax
from jax.experimental import pallas as pl
from jax.experimental.pallas import tpu as pltpu
from jax.sharding import PartitionSpec as P

MESH = pl.DeviceIdType.MESH
PAD = 8
SUB = 32


def tables(points, local, modes):
    width = -(-(2 * modes - 1) // 128) * 128
    mode = np.zeros(width, np.int64)
    mode[:modes] = np.arange(modes)
    mode[modes : 2 * modes - 1] = np.arange(1, modes)

    def rows(index):
        angle = 2.0 * np.pi / points * ((index[:, None] * mode[None, :]) % points)
        out = np.where(np.arange(width) < modes, np.cos(angle), np.sin(angle))
        out[:, 2 * modes - 1 :] = 0.0
        return out

    sectors = points // local
    forward = rows(np.arange(points)).reshape(sectors, local, width)
    scale = np.where(mode == 0, 1.0, 2.0) / points
    scale[2 * modes - 1 :] = 0.0
    return (
        forward.astype(np.float32),
        mode.astype(np.int32),
        scale.astype(np.float32),
    )


def kernel(
    spacing, angle_step, inner,
    dens, velo, pres, weight_in, forward_in,
    dens_out, velo_out, pres_out,
    start, section, halo, halo_next, edge, edge_halo, gathered, pack, from_left, from_right, inv_r,
    weight, forward, inverse,
    load_sem, gather_send, gather_recv, x_send, x_recv, mate_send, mate_recv, hop_send, hop_recv,
    t_send, t_recv,
):
    rows, local = inv_r.shape
    chunks = (rows - inner) // SUB
    tau = 0.05 * spacing
    ax, n_ax = lax.axis_index("ax"), lax.axis_size("ax")
    me = lax.axis_index("sec")
    odd = lax.rem(ax, 2)
    before, after = lax.rem(ax + n_ax - 1, n_ax), lax.rem(ax + 1, n_ax)
    ax_mate = ax + 1 - 2 * odd
    hop_to = lax.rem(ax + 2 - 4 * odd + n_ax, n_ax)
    hop_from = lax.rem(ax - 2 + 4 * odd + n_ax, n_ax)
    left, right = lax.rem(me + 3, 4), lax.rem(me + 1, 4)
    mate = me + 1 - 2 * lax.rem(me, 2)
    opposite = lax.rem(me + 2, 4)
    far = lax.rem(mate + 2, 4)

    whole = pl.ds(PAD, rows)
    loads = [
        pltpu.make_async_copy(dens, start.at[0, :, whole], load_sem.at[0]),
        pltpu.make_async_copy(velo, start.at[1:4, :, whole], load_sem.at[1]),
        pltpu.make_async_copy(pres, start.at[4, :, whole], load_sem.at[2]),
        pltpu.make_async_copy(weight_in, weight, load_sem.at[3]),
        pltpu.make_async_copy(forward_in, forward, load_sem.at[4]),
    ]
    for load in loads:
        load.start()

    barrier = pltpu.get_barrier_semaphore()
    for target in (
        {"ax": before}, {"ax": after}, {"ax": hop_to}, {"ax": hop_from},
        {"sec": mate}, {"sec": opposite}, {"sec": far},
    ):
        pl.semaphore_signal(barrier, inc=1, device_id=target, device_id_type=MESH)
    pl.semaphore_wait(barrier, 7)

    def remote(src, dst, send, recv, target):
        return pltpu.make_async_remote_copy(
            src_ref=src, dst_ref=dst, send_sem=send, recv_sem=recv,
            device_id=target, device_id_type=MESH,
        )

    def inner_copies(stage):
        here = pl.ds(PAD, inner)
        if stage == 0:
            state, low, high = start, halo.at[0, :, 1, here], halo.at[1, :, 0, here]
        else:
            state, low, high = section, halo_next.at[0, :, 0:inner], halo_next.at[1, :, 0:inner]
        return (
            remote(state.at[:, 0, here], high, x_send.at[stage, 0], x_recv.at[stage, 0], {"ax": before}),
            remote(state.at[:, 1, here], low, x_send.at[stage, 1], x_recv.at[stage, 1], {"ax": after}),
        )

    def mate_copy(k):
        here = pl.ds(PAD + inner + k * SUB, SUB)
        return remote(start.at[:, :, here], halo.at[odd, :, :, here],
                      mate_send.at[k], mate_recv.at[k], {"ax": ax_mate})

    def hop_copy(k):
        here = pl.ds(PAD + inner + k * SUB, SUB)
        return remote(halo.at[1 - odd, :, :, here], halo.at[odd, :, :, here],
                      hop_send.at[k], hop_recv.at[k], {"ax": hop_to})

    def t_copies(kind, k):
        return (
            remote(pack.at[kind, k], from_right.at[kind, k],
                   t_send.at[kind, k, 0], t_recv.at[kind, k, 0], {"sec": left}),
            remote(pack.at[kind, k], from_left.at[kind, k],
                   t_send.at[kind, k, 1], t_recv.at[kind, k, 1], {"sec": right}),
        )

    def own_copy(stage, p, way):
        return remote(gathered.at[stage, 0, p], gathered.at[stage, 2 - way, p],
                      gather_send.at[stage, p, way], gather_recv.at[stage, p, way],
                      {"sec": mate if way else opposite})

    def pass_copy(stage, p):
        return remote(gathered.at[stage, 2, p], gathered.at[stage, 3, p],
                      gather_send.at[stage, p, 2], gather_recv.at[stage, p, 2], {"sec": mate})

    sub_lane = lax.broadcasted_iota(jnp.int32, (SUB, local), 1)

    def padded(r0, offset=0):
        return slice(PAD + r0 + offset, PAD + r0 + offset + SUB)

    def first_row(k):
        return inner + k * SUB

    def beside(f, q, where):
        return halo[q, f, 1 - q, where]

    def own(state):
        return lambda f, p, where: state[f, p, where]

    def send_edges(get, kind, k):
        packed = jnp.zeros((SUB, local), jnp.float32)
        for f in range(5):
            for p in range(2):
                i = 2 * f + p
                value = get(f, p, padded(first_row(k)))
                packed = jnp.where(sub_lane == i, pltpu.roll(value, (i + 1) % local, 1), packed)
                packed = jnp.where(sub_lane == 10 + i, pltpu.roll(value, 10 + i, 1), packed)
        pack[kind, k] = packed
        for copy in t_copies(kind, k):
            copy.start()

    def receive_edges(target, kind, k):
        for copy in t_copies(kind, k):
            copy.wait_recv()
        low, high = from_left[kind, k], from_right[kind, k]
        r0 = first_row(k)
        for f in range(5):
            for p in range(2):
                i = 2 * f + p
                a = pltpu.roll(low, (local - i) % local, 1)
                b = pltpu.roll(high, local - 1 - (10 + i), 1)
                target[f, p, r0 : r0 + SUB] = jnp.where(sub_lane == 0, a, b)

    def send_inner(stage, p):
        own_copy(stage, p, 0).start()
        own_copy(stage, p, 1).start()

    def pass_inner(stage, p):
        own_copy(stage, p, 0).wait_recv()
        pass_copy(stage, p).start()

    def back(coeffs, basis):
        return lax.dot_general(coeffs, basis, (((1,), (1,)), ((), ())), precision=lax.Precision.HIGHEST,
                               preferred_element_type=jnp.float32)

    def filter_inner(state, stage):
        for p in range(2):
            own_copy(stage, p, 1).wait_recv()
            pass_copy(stage, p).wait_recv()
            coeffs = None
            for slots, owners in (((0, 1), (me, mate)), ((2, 3), (opposite, far))):
                values = jnp.concatenate([gathered[stage, slots[0], p], gathered[stage, slots[1], p]], axis=1)
                basis = jnp.concatenate([forward[owners[0]], forward[owners[1]]], axis=0)
                part = jnp.dot(values, basis, precision=lax.Precision.HIGHEST, preferred_element_type=jnp.float32)
                coeffs = part if coeffs is None else coeffs + part
            coeffs = coeffs.reshape(5, inner, -1) * weight[...][None]
            flat = coeffs.reshape(5 * inner, -1)
            both = back(flat, inverse[...])
            across = back(coeffs[:, :8].reshape(40, -1), forward[opposite])
            for f in range(5):
                state[f, p, PAD : PAD + inner] = both[f * inner : (f + 1) * inner, :local]
                edge[f, p, 0:inner] = both[f * inner : (f + 1) * inner, local:]
                row = across[8 * f : 8 * f + 1]
                state[f, p, PAD - 1 : PAD] = -row if f in (2, 3) else row
            inner_copies(stage)[p].start()

    def wall(get, put):
        for f in range(5):
            for p in range(2):
                row = get(f, p, slice(PAD + rows - 1, PAD + rows))
                put(f, p, slice(PAD + rows, PAD + rows + 1), -row if f == 2 else row)

    def put_start(f, p, where, row):
        start[f, p, where] = row

    def put_section(f, p, where, row):
        section[f, p, where] = row

    def put_beside(f, q, where, row):
        halo[q, f, 1 - q, where] = row

    def advance(get, p, r0, ahead_x, behind_x, border_ref):
        s = [get(f, p, padded(r0)) for f in range(5)]
        over_r = inv_r[r0 : r0 + SUB]
        over_rho = 1.0 / s[0]
        u, v, w = s[1], s[2], s[3]

        def grads(f):
            gx = ahead_x(f) - behind_x(f)
            gr = get(f, p, padded(r0, 1)) - get(f, p, padded(r0, -1))
            border = border_ref[f, p, r0 : r0 + SUB]
            ahead = jnp.where(sub_lane == local - 1, border, pltpu.roll(s[f], local - 1, 1))
            behind = jnp.where(sub_lane == 0, border, pltpu.roll(s[f], 1, 1))
            gt = (ahead - behind) * ((0.5 / angle_step) * over_r)
            return gx * (0.5 / spacing), gr * (0.5 / spacing), gt

        g = [grads(f) for f in range(5)]
        advect = [u * gx + v * gr + w * gt for gx, gr, gt in g]
        diverg = g[1][0] + g[2][1] + v * over_r + g[3][2]
        rates = (
            -advect[0] - s[0] * diverg,
            -advect[1] - g[4][0] * over_rho,
            -advect[2] + w * w * over_r - g[4][1] * over_rho,
            -advect[3] - v * w * over_r - g[4][2] * over_rho,
            -advect[4] - 1.4 * s[4] * diverg,
        )
        return s, [tau * rate for rate in rates]

    def advance_start(p, r0):
        here = padded(r0)
        if p == 0:
            ahead, behind = (lambda f: start[f, 1, here]), (lambda f: halo[0, f, 1, here])
        else:
            ahead, behind = (lambda f: halo[1, f, 0, here]), (lambda f: start[f, 0, here])
        return advance(own(start), p, r0, ahead, behind, edge)

    def advance_beside(q, r0):
        here = padded(r0)
        if q == 0:
            ahead, behind = (lambda f: start[f, 0, here]), (lambda f: halo[0, f, 0, here])
        else:
            ahead, behind = (lambda f: halo[1, f, 1, here]), (lambda f: start[f, 1, here])
        return advance(beside, q, r0, ahead, behind, edge_halo)

    def finish(p, r0):
        here, plain = padded(r0), slice(r0, r0 + SUB)
        if p == 0:
            ahead, behind = (lambda f: section[f, 1, here]), (lambda f: halo_next[0, f, plain])
        else:
            ahead, behind = (lambda f: halo_next[1, f, plain]), (lambda f: section[f, 0, here])
        s, step = advance(own(section), p, r0, ahead, behind, edge)
        for f in range(5):
            value = 0.5 * start[f, p, here] + 0.5 * (s[f] + step[f])
            target = dens_out if f == 0 else pres_out if f == 4 else velo_out.at[f - 1]
            target[p, plain] = value

    def pass_chunk(k):
        mate_copy(k).wait_recv()
        hop_copy(k).start()

    def take_chunk(k):
        hop_copy(k).wait_recv()
        send_edges(beside, 1, k)
        receive_edges(edge, 0, k)
        r0 = first_row(k)
        for p in range(2):
            s, step = advance_start(p, r0)
            for f in range(5):
                section[f, p, padded(r0)] = s[f] + step[f]
        send_edges(own(section), 2, k)

    def take_beside(k):
        receive_edges(edge_halo, 1, k)
        r0 = first_row(k)
        for q in range(2):
            s, step = advance_beside(q, r0)
            for f in range(5):
                halo_next[q, f, r0 : r0 + SUB] = s[f] + step[f]

    for load in loads[:3]:
        load.wait()
    for p in range(2):
        for f in range(5):
            gathered[0, 0, p, f * inner : (f + 1) * inner] = start[f, p, PAD : PAD + inner]
        send_inner(0, p)
    for k in range(chunks):
        mate_copy(k).start()
    for k in range(chunks):
        send_edges(own(start), 0, k)
    wall(own(start), put_start)
    radius = (lax.broadcasted_iota(jnp.int32, (rows, local), 0).astype(jnp.float32) + 0.5) * spacing
    inv_r[...] = 1.0 / radius
    for load in loads[3:]:
        load.wait()
    inverse[0:local] = forward[me]
    inverse[local : 2 * local] = jnp.zeros((local, inverse.shape[1]), jnp.float32)
    inverse[local : local + 1] = forward[left, local - 1 : local]
    inverse[2 * local - 1 : 2 * local] = forward[right, 0:1]
    for p in range(2):
        pass_inner(0, p)
        pass_chunk(p)
    filter_inner(start, 0)

    for k in range(2, chunks):
        pass_chunk(k)
        take_chunk(k - 2)
    take_chunk(chunks - 2)
    for copy in inner_copies(0):
        copy.wait_recv()
    for p in range(2):
        for r0 in range(0, inner, SUB):
            s, step = advance_start(p, r0)
            for f in range(5):
                gathered[1, 0, p, f * inner + r0 : f * inner + r0 + SUB] = s[f] + step[f]
        send_inner(1, p)
    for k in range(chunks - 2):
        take_beside(k)
    for p in range(2):
        pass_inner(1, p)
    take_chunk(chunks - 1)
    wall(beside, put_beside)
    wall(own(section), put_section)
    for k in range(chunks - 2, chunks):
        take_beside(k)
    filter_inner(section, 1)

    for k in range(chunks):
        receive_edges(edge, 2, k)
        for p in range(2):
            finish(p, first_row(k))
    for copy in inner_copies(1):
        copy.wait_recv()
    for p in range(2):
        for r0 in range(0, inner, SUB):
            finish(p, r0)

    for k in range(chunks):
        mate_copy(k).wait_send()
        hop_copy(k).wait_send()
        for kind in range(3):
            for copy in t_copies(kind, k):
                copy.wait_send()
    for stage in range(2):
        for copy in inner_copies(stage):
            copy.wait_send()
        for p in range(2):
            own_copy(stage, p, 0).wait_send()
            own_copy(stage, p, 1).wait_send()
            pass_copy(stage, p).wait_send()


def body(density, velocity, pressure, cutoff):
    planes, rows, local = density.shape
    points = local * lax.axis_size("sec")
    inner = rows // 4
    forward, mode, scale = tables(points, local, 2 * inner + 1)
    weight = jnp.where(mode[None, :] < cutoff[:, None], scale[None, :], 0.0).astype(jnp.float32)
    f32 = jnp.float32
    chunks = (rows - inner) // SUB
    vmem = pl.BlockSpec(memory_space=pltpu.VMEM)
    hbm = pl.BlockSpec(memory_space=pltpu.MemorySpace.HBM)
    run = pl.pallas_call(
        functools.partial(kernel, 1.0 / rows, 2.0 * math.pi / points, inner),
        out_shape=(
            jax.ShapeDtypeStruct(density.shape, f32),
            jax.ShapeDtypeStruct(velocity.shape, f32),
            jax.ShapeDtypeStruct(pressure.shape, f32),
        ),
        in_specs=[hbm] * 5,
        out_specs=(vmem,) * 3,
        scratch_shapes=[
            pltpu.VMEM((5, planes, rows + 2 * PAD, local), f32),
            pltpu.VMEM((5, planes, rows + 2 * PAD, local), f32),
            pltpu.VMEM((2, 5, planes, rows + 2 * PAD, local), f32),
            pltpu.VMEM((2, 5, rows, local), f32),
            pltpu.VMEM((5, planes, rows, local), f32),
            pltpu.VMEM((5, 2, rows, local), f32),
            pltpu.VMEM((2, 4, planes, 5 * inner, local), f32),
            pltpu.VMEM((3, chunks, SUB, local), f32),
            pltpu.VMEM((3, chunks, SUB, local), f32),
            pltpu.VMEM((3, chunks, SUB, local), f32),
            pltpu.VMEM((rows, local), f32),
            pltpu.VMEM(weight.shape, f32),
            pltpu.VMEM(forward.shape, f32),
            pltpu.VMEM((2 * local, forward.shape[2]), f32),
            pltpu.SemaphoreType.DMA((5,)),
            pltpu.SemaphoreType.DMA((2, planes, 3)),
            pltpu.SemaphoreType.DMA((2, planes, 3)),
            pltpu.SemaphoreType.DMA((2, 2)),
            pltpu.SemaphoreType.DMA((2, 2)),
            pltpu.SemaphoreType.DMA((chunks,)),
            pltpu.SemaphoreType.DMA((chunks,)),
            pltpu.SemaphoreType.DMA((chunks,)),
            pltpu.SemaphoreType.DMA((chunks,)),
            pltpu.SemaphoreType.DMA((3, chunks, 2)),
            pltpu.SemaphoreType.DMA((3, chunks, 2)),
        ],
        compiler_params=pltpu.CompilerParams(
            collective_id=0, has_side_effects=True, vmem_limit_bytes=62 * 1024 * 1024
        ),
    )
    return run(density, velocity, pressure, weight, jnp.asarray(forward))


def solution(mesh):
    return jax.shard_map(
        body,
        mesh=mesh,
        in_specs=(P("ax", None, "sec"), P(None, "ax", None, "sec"), P("ax", None, "sec"), P()),
        out_specs=(P("ax", None, "sec"), P(None, "ax", None, "sec"), P("ax", None, "sec")),
        check_vma=False,
    )
```

time: 77.9 us -> 69 us (0.89)
  the two profiles are of different devices: /device:TPU:0 before, /device:TPU:1 now
where the time goes in v1:
time: 69 us; the launch traced here: 68.8 us
  Pallas kernels  61.6 us (89%)
  local copies, waits for them, and re-layouts  5.16 us (7%)
  other arithmetic  1.4 us (2%)
    pallas_call x1, Pallas kernels, body(): return run(density, velocity, pressure, weight, jnp.asarray(forward))  61.6 us
    unnamed x7, local copies, waits for them, and re-layouts  5.16 us
    select_n x1, other arithmetic, body(): jnp.where(mode[None, :] < cutoff[:, None], scale[None, :], 0.0)  1.4 us

profile of v1, /device:TPU:1, one launch (start us, length us, event | category | flops | bytes accessed | tf_op | source)
XLA Modules:
  0.0 68.8 jit_solution(5972605432904154132)
XLA Ops:
  0.6 0.0 copy-start.1
  0.6 0.7 copy-done.1
  1.3 1.4 %compare_select_fusion.weight_in = f32[64,384]{1,0:T(8,128)} fusion(f32[384]{0:T(512)S(1)} %copy-done.1, s32[384]{0:T(512)} %constant.14, s32[64]{0:T(128)} %param.10), kind=kLoop, calls=%fused_computation | loop fusion | flops 49152 | bytes 101632 | tf_op jit(solution)/shard_map/jit(_where)/select_n | solution.py:368
  2.7 61.6 %shard_map.94 = (f32[2,256,128]{2,1,0:T(8,128)}, f32[3,2,256,128]{3,2,1,0:T(8,128)}, f32[2,256,128]{2,1,0:T(8,128)}) custom-call(f32[2,256,128]{2,1,0:T(8,128)} %dens.1, f32[3,2,256,128]{3,2,1,0:T(8,128)} %velo.1, f32[2,256,128]{2,1,0:T(8,128)} %pres.1, f32[64,384]{1,0:T(8,128)} %compare_select_fusion.weight_in, f32[4,128,384]{2,1,0:T(8,128)} %constant.10.clone.forward_in), custom_call_target="tpu_custom_call" | custom-call | tf_op jit(solution)/shard_map/pallas_call | solution.py:413
  64.3 1.7 %copy.13 = f32[2,256,128]{2,1,0:T(8,128)} copy(f32[2,256,128]{2,1,0:T(8,128)} %get-tuple-element.6) | data formatting | bytes 524288
  66.0 0.0 copy-start
  66.0 2.1 %copy.14 = f32[3,2,256,128]{3,2,1,0:T(8,128)} copy(f32[3,2,256,128]{3,2,1,0:T(8,128)} %get-tuple-element.7) | data formatting | bytes 1572864
  68.1 0.0 copy-done
  68.1 0.7 %copy.15 = f32[2,256,128]{2,1,0:T(8,128)} copy(f32[2,256,128]{2,1,0:T(8,128)S(1)} %copy-done) | data formatting | bytes 524288
Async XLA Ops:
  0.6 0.7 copy-start.1
  66.0 2.1 %copy-start = (f32[2,256,128]{2,1,0:T(8,128)S(1)}, f32[2,256,128]{2,1,0:T(8,128)}, u32[]{:S(2)}) copy-start(f32[2,256,128]{2,1,0:T(8,128)} %get-tuple-element.8) | copy-start | bytes 786436

commit v2 on v1

--- a/solution.py
+++ b/solution.py
@@ -28,18 +28,12 @@
 
     sectors = points // local
     forward = rows(np.arange(points)).reshape(sectors, local, width)
-    scale = np.where(mode == 0, 1.0, 2.0) / points
-    scale[2 * modes - 1 :] = 0.0
-    return (
-        forward.astype(np.float32),
-        mode.astype(np.int32),
-        scale.astype(np.float32),
-    )
+    return forward.astype(np.float32)
 
 
 def kernel(
     spacing, angle_step, inner,
-    dens, velo, pres, weight_in, forward_in,
+    dens, velo, pres, cutoff, forward_in,
     dens_out, velo_out, pres_out,
     start, section, halo, halo_next, edge, edge_halo, gathered, pack, from_left, from_right, inv_r,
     weight, forward, inverse,
@@ -66,8 +60,7 @@
         pltpu.make_async_copy(dens, start.at[0, :, whole], load_sem.at[0]),
         pltpu.make_async_copy(velo, start.at[1:4, :, whole], load_sem.at[1]),
         pltpu.make_async_copy(pres, start.at[4, :, whole], load_sem.at[2]),
-        pltpu.make_async_copy(weight_in, weight, load_sem.at[3]),
-        pltpu.make_async_copy(forward_in, forward, load_sem.at[4]),
+        pltpu.make_async_copy(forward_in, forward, load_sem.at[3]),
     ]
     for load in loads:
         load.start()
@@ -294,28 +287,37 @@
         for f in range(5):
             gathered[0, 0, p, f * inner : (f + 1) * inner] = start[f, p, PAD : PAD + inner]
         send_inner(0, p)
-    for k in range(chunks):
+    early = chunks // 2
+    for k in range(early):
         mate_copy(k).start()
-    for k in range(chunks):
-        send_edges(own(start), 0, k)
     wall(own(start), put_start)
     radius = (lax.broadcasted_iota(jnp.int32, (rows, local), 0).astype(jnp.float32) + 0.5) * spacing
     inv_r[...] = 1.0 / radius
-    for load in loads[3:]:
-        load.wait()
+    loads[3].wait()
     inverse[0:local] = forward[me]
     inverse[local : 2 * local] = jnp.zeros((local, inverse.shape[1]), jnp.float32)
     inverse[local : local + 1] = forward[left, local - 1 : local]
     inverse[2 * local - 1 : 2 * local] = forward[right, 0:1]
+    modes = 2 * inner + 1
+    column = lax.broadcasted_iota(jnp.int32, (1, weight.shape[1]), 1)
+    mode = jnp.where(column < modes, column, column - (modes - 1))
+    scale = jnp.where(column == 0, 1.0 / (4 * local), 2.0 / (4 * local))
+    scale = jnp.where(column < 2 * modes - 1, scale, 0.0)
+    for j in range(inner):
+        weight[j : j + 1] = jnp.where(mode < cutoff[j], scale, 0.0)
     for p in range(2):
         pass_inner(0, p)
         pass_chunk(p)
+    for k in range(chunks):
+        send_edges(own(start), 0, k)
     filter_inner(start, 0)
-
-    for k in range(2, chunks):
+    for k in range(early, chunks):
+        mate_copy(k).start()
+
+    for k in range(2, early):
         pass_chunk(k)
-        take_chunk(k - 2)
-    take_chunk(chunks - 2)
+    for k in range(early):
+        take_chunk(k)
     for copy in inner_copies(0):
         copy.wait_recv()
     for p in range(2):
@@ -324,16 +326,21 @@
             for f in range(5):
                 gathered[1, 0, p, f * inner + r0 : f * inner + r0 + SUB] = s[f] + step[f]
         send_inner(1, p)
-    for k in range(chunks - 2):
+    for k in range(early - 1):
         take_beside(k)
+    pass_chunk(early)
     for p in range(2):
         pass_inner(1, p)
-    take_chunk(chunks - 1)
+        if early + 1 + p < chunks - 1:
+            pass_chunk(early + 1 + p)
+    filter_inner(section, 1)
+    pass_chunk(chunks - 1)
+    for k in range(early, chunks):
+        take_chunk(k)
     wall(beside, put_beside)
     wall(own(section), put_section)
-    for k in range(chunks - 2, chunks):
+    for k in range(early - 1, chunks):
         take_beside(k)
-    filter_inner(section, 1)
 
     for k in range(chunks):
         receive_edges(edge, 2, k)
@@ -364,8 +371,7 @@
     planes, rows, local = density.shape
     points = local * lax.axis_size("sec")
     inner = rows // 4
-    forward, mode, scale = tables(points, local, 2 * inner + 1)
-    weight = jnp.where(mode[None, :] < cutoff[:, None], scale[None, :], 0.0).astype(jnp.float32)
+    forward = tables(points, local, 2 * inner + 1)
     f32 = jnp.float32
     chunks = (rows - inner) // SUB
     vmem = pl.BlockSpec(memory_space=pltpu.VMEM)
@@ -377,7 +383,7 @@
             jax.ShapeDtypeStruct(velocity.shape, f32),
             jax.ShapeDtypeStruct(pressure.shape, f32),
         ),
-        in_specs=[hbm] * 5,
+        in_specs=[hbm] * 3 + [pl.BlockSpec(memory_space=pltpu.SMEM), hbm],
         out_specs=(vmem,) * 3,
         scratch_shapes=[
             pltpu.VMEM((5, planes, rows + 2 * PAD, local), f32),
@@ -391,10 +397,10 @@
             pltpu.VMEM((3, chunks, SUB, local), f32),
             pltpu.VMEM((3, chunks, SUB, local), f32),
             pltpu.VMEM((rows, local), f32),
-            pltpu.VMEM(weight.shape, f32),
+            pltpu.VMEM((inner, forward.shape[2]), f32),
             pltpu.VMEM(forward.shape, f32),
             pltpu.VMEM((2 * local, forward.shape[2]), f32),
-            pltpu.SemaphoreType.DMA((5,)),
+            pltpu.SemaphoreType.DMA((4,)),
             pltpu.SemaphoreType.DMA((2, planes, 3)),
             pltpu.SemaphoreType.DMA((2, planes, 3)),
             pltpu.SemaphoreType.DMA((2, 2)),
@@ -410,7 +416,7 @@
             collective_id=0, has_side_effects=True, vmem_limit_bytes=62 * 1024 * 1024
         ),
     )
-    return run(density, velocity, pressure, weight, jnp.asarray(forward))
+    return run(density, velocity, pressure, cutoff, jnp.asarray(forward))
 
 
 def solution(mesh):

time: 69 us -> 62.1 us (0.900); the launches traced: 68.8 us -> 60.9 us
  Pallas kernels: 61.6 us -> 55.8 us
  other arithmetic: 1.4 us -> 0 us
    pallas_call x1, Pallas kernels: 61.6 us -> 55.8 us  [body(): return run(density, velocity, pressure, cutoff, jnp.asarray(forward))]
    select_n x1 -> x0, other arithmetic: 1.4 us -> none  [body(): jnp.where(mode[None, :] < cutoff[:, None], scale[None, :], 0.0)]
    unnamed x7 -> x5, local copies, waits for them, and re-layouts: 5.16 us -> 4.48 us
where the time goes in v2:
time: 62.1 us; the launch traced here: 60.9 us
  Pallas kernels  55.8 us (90%)
  local copies, waits for them, and re-layouts  4.48 us (7%)
  between operations  0.64 us (1%)
    pallas_call x1, Pallas kernels, body(): return run(density, velocity, pressure, cutoff, jnp.asarray(forward))  55.8 us
    unnamed x5, local copies, waits for them, and re-layouts  4.48 us

profile of v2, /device:TPU:1, one launch (start us, length us, event | category | flops | bytes accessed | tf_op | source)
XLA Modules:
  0.0 60.9 jit_solution(15057494107695744642)
XLA Ops:
  0.6 55.8 %shard_map.76 = (f32[2,256,128]{2,1,0:T(8,128)}, f32[3,2,256,128]{3,2,1,0:T(8,128)}, f32[2,256,128]{2,1,0:T(8,128)}) custom-call(f32[2,256,128]{2,1,0:T(8,128)} %dens.1, f32[3,2,256,128]{3,2,1,0:T(8,128)} %velo.1, f32[2,256,128]{2,1,0:T(8,128)} %pres.1, s32[64]{0:T(128)} %cutoff.1, f32[4,128,384]{2,1,0:T(8,128)} %constant.2.clone.forward_in), custom_call_target="tpu_custom_call" | custom-call | tf_op jit(solution)/shard_map/pallas_call | solution.py:419
  56.4 1.7 %copy.11 = f32[2,256,128]{2,1,0:T(8,128)} copy(f32[2,256,128]{2,1,0:T(8,128)} %get-tuple-element.6) | data formatting | bytes 524288
  58.1 0.0 copy-start
  58.1 2.1 %copy.12 = f32[3,2,256,128]{3,2,1,0:T(8,128)} copy(f32[3,2,256,128]{3,2,1,0:T(8,128)} %get-tuple-element.7) | data formatting | bytes 1572864
  60.2 0.0 copy-done
  60.2 0.7 %copy.13 = f32[2,256,128]{2,1,0:T(8,128)} copy(f32[2,256,128]{2,1,0:T(8,128)S(1)} %copy-done) | data formatting | bytes 524288
Async XLA Ops:
  58.1 2.1 %copy-start = (f32[2,256,128]{2,1,0:T(8,128)S(1)}, f32[2,256,128]{2,1,0:T(8,128)}, u32[]{:S(2)}) copy-start(f32[2,256,128]{2,1,0:T(8,128)} %get-tuple-element.8) | copy-start | bytes 786436

commit v3 on v2

--- a/solution.py
+++ b/solution.py
@@ -36,7 +36,7 @@
     dens, velo, pres, cutoff, forward_in,
     dens_out, velo_out, pres_out,
     start, section, halo, halo_next, edge, edge_halo, gathered, pack, from_left, from_right, inv_r,
-    weight, forward, inverse,
+    weight, forward, inverse, basis_high, basis_low, inverse_high, inverse_low,
     load_sem, gather_send, gather_recv, x_send, x_recv, mate_send, mate_recv, hop_send, hop_recv,
     t_send, t_recv,
 ):
@@ -139,14 +139,21 @@
                 value = get(f, p, padded(first_row(k)))
                 packed = jnp.where(sub_lane == i, pltpu.roll(value, (i + 1) % local, 1), packed)
                 packed = jnp.where(sub_lane == 10 + i, pltpu.roll(value, 10 + i, 1), packed)
-        pack[kind, k] = packed
+        folded = packed[0:8]
+        for g in range(1, SUB // 8):
+            folded = folded + pltpu.roll(packed[8 * g : 8 * g + 8], 32 * g, 1)
+        pack[kind, k] = folded
         for copy in t_copies(kind, k):
             copy.start()
+
+    def unfolded(value):
+        parts = [value] + [pltpu.roll(value, local - 32 * g, 1) for g in range(1, SUB // 8)]
+        return jnp.concatenate(parts, axis=0)
 
     def receive_edges(target, kind, k):
         for copy in t_copies(kind, k):
             copy.wait_recv()
-        low, high = from_left[kind, k], from_right[kind, k]
+        low, high = unfolded(from_left[kind, k]), unfolded(from_right[kind, k])
         r0 = first_row(k)
         for f in range(5):
             for p in range(2):
@@ -163,24 +170,29 @@
         own_copy(stage, p, 0).wait_recv()
         pass_copy(stage, p).start()
 
-    def back(coeffs, basis):
-        return lax.dot_general(coeffs, basis, (((1,), (1,)), ((), ())), precision=lax.Precision.HIGHEST,
-                               preferred_element_type=jnp.float32)
+    def halves(value):
+        high = value.astype(jnp.bfloat16)
+        return high, (value - high.astype(jnp.float32)).astype(jnp.bfloat16)
+
+    def product(value, basis_high, basis_low, dim):
+        high, low = halves(value)
+
+        def dot(a, b):
+            return lax.dot_general(a, b, (((1,), (dim,)), ((), ())), preferred_element_type=jnp.float32)
+
+        return dot(high, basis_high) + (dot(high, basis_low) + dot(low, basis_high))
 
     def filter_inner(state, stage):
         for p in range(2):
             own_copy(stage, p, 1).wait_recv()
             pass_copy(stage, p).wait_recv()
-            coeffs = None
-            for slots, owners in (((0, 1), (me, mate)), ((2, 3), (opposite, far))):
-                values = jnp.concatenate([gathered[stage, slots[0], p], gathered[stage, slots[1], p]], axis=1)
-                basis = jnp.concatenate([forward[owners[0]], forward[owners[1]]], axis=0)
-                part = jnp.dot(values, basis, precision=lax.Precision.HIGHEST, preferred_element_type=jnp.float32)
-                coeffs = part if coeffs is None else coeffs + part
+            values = jnp.concatenate([gathered[stage, slot, p] for slot in range(4)], axis=1)
+            coeffs = product(values, basis_high[...], basis_low[...], 0)
             coeffs = coeffs.reshape(5, inner, -1) * weight[...][None]
             flat = coeffs.reshape(5 * inner, -1)
-            both = back(flat, inverse[...])
-            across = back(coeffs[:, :8].reshape(40, -1), forward[opposite])
+            both = product(flat, inverse_high[...], inverse_low[...], 1)
+            across = product(coeffs[:, :8].reshape(40, -1), basis_high[2 * local : 3 * local],
+                             basis_low[2 * local : 3 * local], 1)
             for f in range(5):
                 state[f, p, PAD : PAD + inner] = both[f * inner : (f + 1) * inner, :local]
                 edge[f, p, 0:inner] = both[f * inner : (f + 1) * inner, local:]
@@ -298,6 +310,10 @@
     inverse[local : 2 * local] = jnp.zeros((local, inverse.shape[1]), jnp.float32)
     inverse[local : local + 1] = forward[left, local - 1 : local]
     inverse[2 * local - 1 : 2 * local] = forward[right, 0:1]
+    inverse_high[...], inverse_low[...] = halves(inverse[...])
+    for slot, owner in enumerate((me, mate, opposite, far)):
+        span = slice(slot * local, (slot + 1) * local)
+        basis_high[span], basis_low[span] = halves(forward[owner])
     modes = 2 * inner + 1
     column = lax.broadcasted_iota(jnp.int32, (1, weight.shape[1]), 1)
     mode = jnp.where(column < modes, column, column - (modes - 1))
@@ -393,13 +409,17 @@
             pltpu.VMEM((5, planes, rows, local), f32),
             pltpu.VMEM((5, 2, rows, local), f32),
             pltpu.VMEM((2, 4, planes, 5 * inner, local), f32),
-            pltpu.VMEM((3, chunks, SUB, local), f32),
-            pltpu.VMEM((3, chunks, SUB, local), f32),
-            pltpu.VMEM((3, chunks, SUB, local), f32),
+            pltpu.VMEM((3, chunks, 8, local), f32),
+            pltpu.VMEM((3, chunks, 8, local), f32),
+            pltpu.VMEM((3, chunks, 8, local), f32),
             pltpu.VMEM((rows, local), f32),
             pltpu.VMEM((inner, forward.shape[2]), f32),
             pltpu.VMEM(forward.shape, f32),
             pltpu.VMEM((2 * local, forward.shape[2]), f32),
+            pltpu.VMEM((points, forward.shape[2]), jnp.bfloat16),
+            pltpu.VMEM((points, forward.shape[2]), jnp.bfloat16),
+            pltpu.VMEM((2 * local, forward.shape[2]), jnp.bfloat16),
+            pltpu.VMEM((2 * local, forward.shape[2]), jnp.bfloat16),
             pltpu.SemaphoreType.DMA((4,)),
             pltpu.SemaphoreType.DMA((2, planes, 3)),
             pltpu.SemaphoreType.DMA((2, planes, 3)),

time: 62.1 us -> 59.3 us (0.955); the launches traced: 60.9 us -> 59.1 us
  Pallas kernels: 55.8 us -> 54 us
    pallas_call x1, Pallas kernels: 55.8 us -> 54 us  [body(): return run(density, velocity, pressure, cutoff, jnp.asarray(forward))]
where the time goes in v3:
time: 59.3 us; the launch traced here: 59.1 us
  Pallas kernels  54 us (91%)
  local copies, waits for them, and re-layouts  4.48 us (8%)
  between operations  0.64 us (1%)
    pallas_call x1, Pallas kernels, body(): return run(density, velocity, pressure, cutoff, jnp.asarray(forward))  54 us
    unnamed x5, local copies, waits for them, and re-layouts  4.48 us

profile of v3, /device:TPU:1, one launch (start us, length us, event | category | flops | bytes accessed | tf_op | source)
XLA Modules:
  0.0 59.1 jit_solution(17416838499006151350)
XLA Ops:
  0.6 54.0 %shard_map.76 = (f32[2,256,128]{2,1,0:T(8,128)}, f32[3,2,256,128]{3,2,1,0:T(8,128)}, f32[2,256,128]{2,1,0:T(8,128)}) custom-call(f32[2,256,128]{2,1,0:T(8,128)} %dens.1, f32[3,2,256,128]{3,2,1,0:T(8,128)} %velo.1, f32[2,256,128]{2,1,0:T(8,128)} %pres.1, s32[64]{0:T(128)} %cutoff.1, f32[4,128,384]{2,1,0:T(8,128)} %constant.2.clone.forward_in), custom_call_target="tpu_custom_call" | custom-call | tf_op jit(solution)/shard_map/pallas_call | solution.py:439
  54.7 1.7 %copy.11 = f32[2,256,128]{2,1,0:T(8,128)} copy(f32[2,256,128]{2,1,0:T(8,128)} %get-tuple-element.6) | data formatting | bytes 524288
  56.3 0.0 copy-start
  56.3 2.1 %copy.12 = f32[3,2,256,128]{3,2,1,0:T(8,128)} copy(f32[3,2,256,128]{3,2,1,0:T(8,128)} %get-tuple-element.7) | data formatting | bytes 1572864
  58.4 0.0 copy-done
  58.4 0.7 %copy.13 = f32[2,256,128]{2,1,0:T(8,128)} copy(f32[2,256,128]{2,1,0:T(8,128)S(1)} %copy-done) | data formatting | bytes 524288
Async XLA Ops:
  56.3 2.1 %copy-start = (f32[2,256,128]{2,1,0:T(8,128)S(1)}, f32[2,256,128]{2,1,0:T(8,128)}, u32[]{:S(2)}) copy-start(f32[2,256,128]{2,1,0:T(8,128)} %get-tuple-element.8) | copy-start | bytes 786436

commit v4 on v3

--- a/solution.py
+++ b/solution.py
@@ -302,6 +302,8 @@
     early = chunks // 2
     for k in range(early):
         mate_copy(k).start()
+    for k in range(chunks):
+        send_edges(own(start), 0, k)
     wall(own(start), put_start)
     radius = (lax.broadcasted_iota(jnp.int32, (rows, local), 0).astype(jnp.float32) + 0.5) * spacing
     inv_r[...] = 1.0 / radius
@@ -324,8 +326,6 @@
     for p in range(2):
         pass_inner(0, p)
         pass_chunk(p)
-    for k in range(chunks):
-        send_edges(own(start), 0, k)
     filter_inner(start, 0)
     for k in range(early, chunks):
         mate_copy(k).start()

time: 59.3 us -> 59.6 us (level); the launches traced: 59.1 us -> 58.6 us
  no operation moved by 1% of the time
where the time goes in v4:
time: 59.6 us; the launch traced here: 58.6 us
  Pallas kernels  53.5 us (90%)
  local copies, waits for them, and re-layouts  4.48 us (8%)
  between operations  0.64 us (1%)
    pallas_call x1, Pallas kernels, body(): return run(density, velocity, pressure, cutoff, jnp.asarray(forward))  53.5 us
    unnamed x5, local copies, waits for them, and re-layouts  4.48 us

profile of v4, /device:TPU:1, one launch (start us, length us, event | category | flops | bytes accessed | tf_op | source)
XLA Modules:
  0.0 58.6 jit_solution(13497267872125357550)
XLA Ops:
  0.6 53.5 %shard_map.76 = (f32[2,256,128]{2,1,0:T(8,128)}, f32[3,2,256,128]{3,2,1,0:T(8,128)}, f32[2,256,128]{2,1,0:T(8,128)}) custom-call(f32[2,256,128]{2,1,0:T(8,128)} %dens.1, f32[3,2,256,128]{3,2,1,0:T(8,128)} %velo.1, f32[2,256,128]{2,1,0:T(8,128)} %pres.1, s32[64]{0:T(128)} %cutoff.1, f32[4,128,384]{2,1,0:T(8,128)} %constant.2.clone.forward_in), custom_call_target="tpu_custom_call" | custom-call | tf_op jit(solution)/shard_map/pallas_call | solution.py:439
  54.1 1.7 %copy.11 = f32[2,256,128]{2,1,0:T(8,128)} copy(f32[2,256,128]{2,1,0:T(8,128)} %get-tuple-element.6) | data formatting | bytes 524288
  55.8 0.0 copy-start
  55.8 2.1 %copy.12 = f32[3,2,256,128]{3,2,1,0:T(8,128)} copy(f32[3,2,256,128]{3,2,1,0:T(8,128)} %get-tuple-element.7) | data formatting | bytes 1572864
  57.9 0.0 copy-done
  57.9 0.7 %copy.13 = f32[2,256,128]{2,1,0:T(8,128)} copy(f32[2,256,128]{2,1,0:T(8,128)S(1)} %copy-done) | data formatting | bytes 524288
Async XLA Ops:
  55.8 2.1 %copy-start = (f32[2,256,128]{2,1,0:T(8,128)S(1)}, f32[2,256,128]{2,1,0:T(8,128)}, u32[]{:S(2)}) copy-start(f32[2,256,128]{2,1,0:T(8,128)} %get-tuple-element.8) | copy-start | bytes 786436
